TPU v7x, 32 devices: a whole 2x2x4 slice. The times are simulated.
32 devices in a mesh: groups: 2 (over x), row: 16 (over z, y, core).
Axes of the slice: x: 2, y: 2, z: 4, core: 2. Of those that a mesh axis runs over, the one named last changes fastest.
Arguments:
- inverse: float32 [4, 4096, 4096], P('groups', 'row'), parts along dimension 0, as said below
- cycle: bfloat16 [4, 4096, 1024], P('groups', 'row'), parts along dimension 0, as said below
- arrivals: bfloat16 [4, 2, 4096, 128], P('groups', None, 'row'), parts along dimension 0, may hold values from -6 to 6
- departing: int32 [4, 128], P('groups'), parts along dimension 0, may hold values from 0 to 1023, as said below
- directions: int32 [4, 512], P('groups'), parts along dimension 0, may hold values from 0 to 8191
Outputs:
- new_inverse: float32 [4, 4096, 4096], P('groups', 'row'), parts along dimension 0
- beam_weights: float32 [4, 2, 4096, 512], P('groups', None, 'row'), parts along dimension 0
- spectrum: float32 [4, 512], P('groups'), parts along dimension 0
There are 2 independent parts, one for each index of `groups`. A program takes and returns all parts, laid end to end along the dimension named above; each array names one. Nothing has to cross between parts.
Inputs may be any that keep to these rules, and one draw needn't show every extreme that they name: inverse is Hermitian and is the inverse of I + cycle cycle^H / 1024. `cycle`: the snapshots whose inverse covariance is given. `departing`: all 2 x 128 entries are different slots.
All inputs are finite; a program needn't handle non-finite values.
Results may differ from a plain program's by a relative error of at most 0.0003.
Values may be sent and summed in bfloat16 or wider, within the bound.
No kernel may reach another device: no remote copies, remote signals or barrier semaphores. Data moves between devices by JAX's collectives and lax.ppermute only.
A program may use at most 192 MiB of HBM per device.

v0:
```python
import jax
import jax.numpy as jnp
from jax import lax
from jax.sharding import PartitionSpec as P

M = 4096
CYCLE = 1024
STEPS = 2
precise = lax.Precision.HIGHEST


def matmul(left, right):
    return jnp.dot(left, right, precision=precise, preferred_element_type=jnp.float32)


def lead_dot(left, right):
    return lax.dot_general(
        left, right, (((0,), (0,)), ((), ())), precision=precise, preferred_element_type=jnp.float32
    )


def tail_dot(left, right):
    return lax.dot_general(
        left, right, (((1,), (1,)), ((), ())), precision=precise, preferred_element_type=jnp.float32
    )


def complex_mul(left_re, left_im, right_re, right_im):
    return (
        matmul(left_re, right_re) - matmul(left_im, right_im),
        matmul(left_re, right_im) + matmul(left_im, right_re),
    )


def steering(direction_ids, length):
    element = jnp.arange(length, dtype=jnp.int32)[:, None]
    odd_index = 2 * direction_ids[None, :] + 1
    angle_count = 2 * length
    turns = (element * odd_index - element * angle_count) % (2 * angle_count)
    phase = jnp.pi * turns.astype(jnp.float32) / angle_count
    return (jnp.cos(phase), jnp.sin(phase))


def hermitian_solve(herm_re, herm_im, rhs_re, rhs_im):
    order = herm_re.shape[0]
    embedded = jnp.concatenate(
        [jnp.concatenate([herm_re, -herm_im], 1), jnp.concatenate([herm_im, herm_re], 1)], 0
    )
    factor = jnp.linalg.cholesky(embedded)
    solution = jax.scipy.linalg.cho_solve((factor, True), jnp.concatenate([rhs_re, rhs_im], 0))
    return (solution[:order], solution[order:])


def block_product(current, snap_block):
    inv_re, inv_im = current
    piece_wide = lax.all_gather(snap_block, "row", axis=1, tiled=True).astype(jnp.float32)
    new_re = matmul(inv_re, piece_wide[0]) - matmul(inv_im, piece_wide[1])
    new_im = matmul(inv_re, piece_wide[1]) + matmul(inv_im, piece_wide[0])
    return (new_re, new_im)


def capacitance(snap_block, q_re, q_im):
    snap_wide = snap_block.astype(jnp.float32)
    cap_re = lead_dot(snap_wide[0], q_re) + lead_dot(snap_wide[1], q_im)
    cap_im = lead_dot(snap_wide[0], q_im) - lead_dot(snap_wide[1], q_re)
    return lax.psum((cap_re, cap_im), "row")


def apply_update(current, q_re, q_im, fold_re, fold_im):
    inv_re, inv_im = current
    shard_piece = lax.all_gather(jnp.stack([q_re, q_im]), "row", axis=1, tiled=True)
    new_re = inv_re - tail_dot(fold_re, shard_piece[0]) - tail_dot(fold_im, shard_piece[1])
    new_im = inv_im - tail_dot(fold_im, shard_piece[0]) + tail_dot(fold_re, shard_piece[1])
    updated = jnp.stack([new_re, new_im])
    return (updated[0], updated[1])


def joint_update(current, snap_block):
    q_re, q_im = block_product(current, snap_block)
    cap_re, cap_im = capacitance(snap_block, q_re, q_im)
    half = snap_block.shape[2] // 2
    identity = CYCLE * jnp.eye(half, dtype=jnp.float32)
    rhs_re, rhs_im = (q_re.T, -q_im.T)
    col_count = rhs_re.shape[1]
    first_re, first_im = hermitian_solve(
        identity + cap_re[:half, :half],
        cap_im[:half, :half],
        jnp.concatenate([rhs_re[:half], cap_re[:half, half:]], 1),
        jnp.concatenate([rhs_im[:half], cap_im[:half, half:]], 1),
    )
    base_re, base_im = (first_re[:, :col_count], first_im[:, :col_count])
    cross_re, cross_im = (first_re[:, col_count:], first_im[:, col_count:])
    prod_re, prod_im = complex_mul(cap_re[half:, :half], cap_im[half:, :half], cross_re, cross_im)
    schur_re = identity - cap_re[half:, half:] + prod_re
    schur_im = -cap_im[half:, half:] + prod_im
    lower_re, lower_im = complex_mul(cap_re[half:, :half], cap_im[half:, :half], base_re, base_im)
    second_re, second_im = hermitian_solve(
        schur_re, schur_im, rhs_re[half:] - lower_re, rhs_im[half:] - lower_im
    )
    upper_re, upper_im = complex_mul(cross_re, cross_im, -second_re, -second_im)
    sol_re = jnp.concatenate([base_re - upper_re, -second_re], 0)
    sol_im = jnp.concatenate([base_im - upper_im, -second_im], 0)
    return apply_update(current, q_re, q_im, sol_re.T, -sol_im.T)


def on_device(inverse, cycle, arrivals, departing, directions):
    current = (inverse[0], inverse[1])
    row_count = inverse.shape[1]
    first_row = lax.axis_index("row") * row_count
    weight_list = []
    power_list = []
    for step_index in range(STEPS):
        steer_re, steer_im = steering(directions[step_index], M)
        local_re = lax.dynamic_slice_in_dim(steer_re, first_row, row_count, 0)
        local_im = lax.dynamic_slice_in_dim(steer_im, first_row, row_count, 0)
        app_re, app_im = complex_mul(current[0], current[1], steer_re, steer_im)
        partial_power = jnp.sum(local_re * app_re + local_im * app_im, axis=0)
        power = lax.psum(partial_power, "row")
        departed = jnp.take(cycle, departing[step_index], axis=2)
        current = joint_update(current, jnp.concatenate([arrivals[step_index], departed], axis=2))
        weight_list.append(jnp.stack([M * app_re / power, M * app_im / power]))
        power_list.append(M / power)
    return (jnp.stack([current[0], current[1]]), jnp.stack(weight_list), jnp.stack(power_list))


def solution(mesh):
    in_specs = (
        P("groups", "row", None),
        P("groups", "row", None),
        P("groups", None, "row", None),
        P("groups", None),
        P("groups", None),
    )
    out_specs = (P("groups", "row", None), P("groups", None, "row", None), P("groups", None))
    return jax.shard_map(
        on_device, mesh=mesh, in_specs=in_specs, out_specs=out_specs, check_vma=False
    )
```

profile of v0, /device:TPU:0, one launch (start us, length us, event | category | flops | bytes accessed | tf_op | source)
XLA Modules:
  0.0 946.1 jit_solution(2639609312674014120)
XLA Ops:
  26.9 44.0 %fusion.14 = f32[512,256]{0,1:T(8,128)S(1)} fusion(s32[4096]{0:T(1024)S(1)} %iota_multiply_fusion, s32[512]{0:T(512)S(1)} %bitcast.363, f32[256,4096]{1,0:T(8,128)} %fusion.361), kind=kOutput, calls=%fused_computation.43 | convolution fusion | flops 6473908224 | bytes 4737024 | tf_op jit(solution)/shard_map/dot_general | solution.py:13
  71.0 52.9 %fusion.12 = f32[512,256]{0,1:T(8,128)} fusion(s32[4096]{0:T(1024)S(1)} %iota_multiply_fusion, s32[512]{0:T(512)S(1)} %bitcast.364, f32[256,4096]{1,0:T(8,128)S(1)} %copy-done.11), kind=kOutput, calls=%fused_computation.41 | convolution fusion | flops 6473908224 | bytes 4737024 | tf_op jit(solution)/shard_map/dot_general | solution.py:13
  123.8 52.9 %fusion.71 = f32[256,512]{1,0:T(8,128)} fusion(f32[512,256]{0,1:T(8,128)S(1)} %fusion.14, s32[4096]{0:T(1024)S(1)} %iota_multiply_fusion, s32[512]{0:T(512)S(1)} %bitcast.365, f32[256,4096]{1,0:T(8,128)S(1)} %copy-done.10), kind=kOutput, calls=%fused_computation.85 | convolution fusion | flops 6474039296 | bytes 5261312 | tf_op jit(solution)/shard_map/dot_general | solution.py:13
  176.7 14.3 %fusion.275 = (bf16[1,4096,256]{1,0,2:T(2,128)(2,1)}, bf16[1,4096,256]{1,0,2:T(2,128)(2,1)}) fusion(bf16[2,4096,256]{1,0,2:T(2,128)(2,1)} %all-gather.5.cloned.1.call-done), kind=kLoop, calls=%fused_computation.391 | loop fusion | bytes 8388608 | tf_op jit(solution)/shard_map/slice | solution.py:57
  191.1 9.7 %copy.51 = bf16[1,4096,256]{2,1,0:T(8,128)(2,1)} copy(bf16[1,4096,256]{1,0,2:T(2,128)(2,1)} %get-tuple-element.92) | data formatting | bytes 4194304 | tf_op jit(solution)/shard_map/slice | solution.py:57
  237.1 68.7 %fusion.11 = (f32[4096,512]{1,0:T(8,128)S(1)}, f32[4096,512]{1,0:T(8,128)S(1)}, f32[4096,512]{1,0:T(8,128)}, f32[4096,512]{1,0:T(8,128)}) fusion(s32[4096]{0:T(1024)S(1)} %iota_multiply_fusion, s32[512]{0:T(512)S(1)} %bitcast.366, s32[512]{0:T(512)S(1)} %bitcast.358), kind=kLoop, calls=%fused_computation.36 | loop fusion | flops 62914560 | bytes 33574912 | tf_op jit(solution)/shard_map/cos | solution.py:41
  305.8 40.4 %add_reduce_fusion.1 = (f32[512]{0:T(512)}, f32[256,512]{1,0:T(8,128)}) fusion(f32[4096,512]{1,0:T(8,128)S(1)} %get-tuple-element.126, s32[]{:T(128)S(6)} %select_n.28, f32[256,512]{1,0:T(8,128)S(1)} %copy-done.19, f32[4096,512]{1,0:T(8,128)S(1)} %get-tuple-element.125, f32[512,256]{0,1:T(8,128)S(1)} %copy-done.28, s32[4096]{0:T(1024)S(1)} %iota_multiply_fusion, ...), kind=kOutput, calls=%fused_computation.143 | convolution fusion | flops 6474563072 | bytes 6836228 | tf_op jit(solution)/shard_map/dot_general | solution.py:13
  346.9 11.6 %fusion.274 = (bf16[1,4096,256]{1,0,2:T(2,128)(2,1)}, bf16[1,4096,256]{1,0,2:T(2,128)(2,1)}) fusion(bf16[2,4096,256]{1,0,2:T(2,128)(2,1)} %all-gather.9.cloned.1.call-done), kind=kLoop, calls=%fused_computation.390 | loop fusion | bytes 8388608 | tf_op jit(solution)/shard_map/slice | solution.py:57
  358.5 9.3 copy.66
  367.8 9.7 %copy.65 = bf16[1,4096,256]{2,1,0:T(8,128)(2,1)} copy(bf16[1,4096,256]{1,0,2:T(2,128)(2,1)} %get-tuple-element.89) | data formatting | bytes 4194304 | tf_op jit(solution)/shard_map/slice | solution.py:57
  379.4 11.7 %cholesky.214 = f32[128,128]{1,0:T(8,128)S(1)} custom-call(f32[128,128]{1,0:T(8,128)S(1)} %cholesky.346), custom_call_target="Cholesky" | custom-call | tf_op jit(solution)/shard_map/jit(cholesky)/cholesky | solution.py:49
  391.2 9.8 %custom-call.23 = f32[1,128,128]{1,2,0:T(8,128)S(1)} custom-call(f32[1,128,128]{2,1,0:T(8,128)S(1)} %get-tuple-element.124), custom_call_target="InvertDiagBlocksLowerTriangular" | custom-call | tf_op jit(solution)/shard_map/jit(cholesky)/cholesky | solution.py:49
  401.5 11.7 %cholesky.231 = f32[128,128]{1,0:T(8,128)S(1)} custom-call(f32[128,128]{1,0:T(8,128)S(1)} %convolution_subtract_fusion.25), custom_call_target="Cholesky" | custom-call | tf_op jit(solution)/shard_map/jit(cholesky)/cholesky | solution.py:49
  420.5 20.1 %custom-call.24 = f32[2,128,128]{1,2,0:T(8,128)S(1)} custom-call(f32[2,128,128]{2,1,0:T(8,128)S(1)} %get-tuple-element.35), custom_call_target="InvertDiagBlocksLowerTriangular" | custom-call | tf_op jit(solution)/shard_map/jit(_cho_solve)/triangular_solve | solution.py:50
  452.6 11.7 %cholesky.248 = f32[128,128]{1,0:T(8,128)S(1)} custom-call(f32[128,128]{1,0:T(8,128)S(1)} %cholesky.349), custom_call_target="Cholesky" | custom-call | tf_op jit(solution)/shard_map/jit(cholesky)/cholesky | solution.py:49
  464.4 9.8 %custom-call.25 = f32[1,128,128]{1,2,0:T(8,128)S(1)} custom-call(f32[1,128,128]{2,1,0:T(8,128)S(1)} %get-tuple-element.120), custom_call_target="InvertDiagBlocksLowerTriangular" | custom-call | tf_op jit(solution)/shard_map/jit(cholesky)/cholesky | solution.py:49
  476.3 11.9 %cholesky.265 = f32[128,128]{1,0:T(8,128)S(1)} custom-call(f32[128,128]{1,0:T(8,128)S(1)} %convolution_subtract_fusion.23), custom_call_target="Cholesky" | custom-call | tf_op jit(solution)/shard_map/jit(cholesky)/cholesky | solution.py:49
  496.8 19.7 %custom-call.26 = f32[2,128,128]{1,2,0:T(8,128)S(1)} custom-call(f32[2,128,128]{2,1,0:T(8,128)S(1)} %get-tuple-element.36), custom_call_target="InvertDiagBlocksLowerTriangular" | custom-call | tf_op jit(solution)/shard_map/jit(_cho_solve)/triangular_solve | solution.py:50
  535.6 39.2 %fusion.30 = f32[256,512]{1,0:T(8,128)} fusion(f32[256,4096]{1,0:T(8,128)S(1)} %convolution_subtract_fusion.4, s32[512]{0:T(512)S(1)} %bitcast.359, s32[4096]{0:T(1024)S(1)} %iota_multiply_fusion), kind=kOutput, calls=%fused_computation.58 | convolution fusion | flops 6473908224 | bytes 4737024 | tf_op jit(solution)/shard_map/dot_general | solution.py:13
  595.2 43.5 %fusion.28 = f32[256,512]{1,0:T(8,128)S(1)} fusion(f32[256,4096]{1,0:T(8,128)} %copy-done.3, s32[512]{0:T(512)S(1)} %bitcast.360, s32[4096]{0:T(1024)S(1)} %iota_multiply_fusion), kind=kOutput, calls=%fused_computation.57 | convolution fusion | flops 6473908224 | bytes 4737024 | tf_op jit(solution)/shard_map/dot_general | solution.py:13
  638.7 38.5 %fusion.60 = f32[256,512]{1,0:T(8,128)S(1)} fusion(f32[256,512]{1,0:T(8,128)S(1)} %copy-done.29, f32[256,4096]{1,0:T(8,128)S(1)} %copy-done.4, s32[512]{0:T(512)S(1)} %bitcast.361, s32[4096]{0:T(1024)S(1)} %iota_multiply_fusion), kind=kOutput, calls=%fused_computation.82 | convolution fusion | flops 6474039296 | bytes 5261312 | tf_op jit(solution)/shard_map/dot_general | solution.py:13
  677.2 53.5 %add_reduce_fusion = (f32[512]{0:T(512)S(1)}, f32[256,512]{1,0:T(8,128)S(1)}) fusion(f32[4096,512]{1,0:T(8,128)} %get-tuple-element.129, s32[]{:T(128)S(6)} %select_n.28, f32[256,512]{1,0:T(8,128)S(1)} %fusion.60, f32[4096,512]{1,0:T(8,128)} %get-tuple-element.130, f32[256,512]{1,0:T(8,128)S(1)} %fusion.28, f32[256,4096]{1,0:T(8,128)S(1)} %copy-done.2, ...), kind=kOutput, calls=%fused_computation.140 | convolution fusion | flops 6474563072 | bytes 6836228 | tf_op jit(solution)/shard_map/dot_general | solution.py:13
  730.7 36.4 %all-reduce.1 = (f32[512]{0:T(512)S(1)}, f32[512]{0:T(512)S(1)}) all-reduce(f32[512]{0:T(512)S(1)} %get-tuple-element.157, f32[512]{0:T(512)S(1)} %copy-done.25), channel_id=1, replica_groups=mesh['groups'=2,'row'=16] {'row'}, use_global_device_ids=true, to_apply=%region_11.16 | all-reduce | flops 1024 | bytes 8192 | tf_op jit(solution)/shard_map/psum | solution.py:118
  771.8 11.7 %cholesky.282 = f32[128,128]{1,0:T(8,128)S(1)} custom-call(f32[128,128]{1,0:T(8,128)S(1)} %cholesky.352), custom_call_target="Cholesky" | custom-call | tf_op jit(solution)/shard_map/jit(cholesky)/cholesky | solution.py:49
  783.6 9.8 %custom-call.27 = f32[1,128,128]{1,2,0:T(8,128)S(1)} custom-call(f32[1,128,128]{2,1,0:T(8,128)S(1)} %get-tuple-element.116), custom_call_target="InvertDiagBlocksLowerTriangular" | custom-call | tf_op jit(solution)/shard_map/jit(cholesky)/cholesky | solution.py:49
  793.9 11.7 %cholesky.299 = f32[128,128]{1,0:T(8,128)S(1)} custom-call(f32[128,128]{1,0:T(8,128)S(1)} %convolution_subtract_fusion.22), custom_call_target="Cholesky" | custom-call | tf_op jit(solution)/shard_map/jit(cholesky)/cholesky | solution.py:49
  812.5 19.8 %custom-call.28 = f32[2,128,128]{1,2,0:T(8,128)S(1)} custom-call(f32[2,128,128]{2,1,0:T(8,128)S(1)} %get-tuple-element.37), custom_call_target="InvertDiagBlocksLowerTriangular" | custom-call | tf_op jit(solution)/shard_map/jit(_cho_solve)/triangular_solve | solution.py:50
  837.0 11.7 %cholesky.316 = f32[128,128]{1,0:T(8,128)S(1)} custom-call(f32[128,128]{1,0:T(8,128)S(1)} %cholesky.355), custom_call_target="Cholesky" | custom-call | tf_op jit(solution)/shard_map/jit(cholesky)/cholesky | solution.py:49
  848.7 9.8 %custom-call.29 = f32[1,128,128]{1,2,0:T(8,128)S(1)} custom-call(f32[1,128,128]{2,1,0:T(8,128)S(1)} %get-tuple-element.112), custom_call_target="InvertDiagBlocksLowerTriangular" | custom-call | tf_op jit(solution)/shard_map/jit(cholesky)/cholesky | solution.py:49
  859.0 11.9 %cholesky.333 = f32[128,128]{1,0:T(8,128)S(1)} custom-call(f32[128,128]{1,0:T(8,128)S(1)} %convolution_subtract_fusion.20), custom_call_target="Cholesky" | custom-call | tf_op jit(solution)/shard_map/jit(cholesky)/cholesky | solution.py:49
  877.8 19.7 %custom-call.30 = f32[2,128,128]{1,2,0:T(8,128)S(1)} custom-call(f32[2,128,128]{2,1,0:T(8,128)S(1)} %get-tuple-element.38), custom_call_target="InvertDiagBlocksLowerTriangular" | custom-call | tf_op jit(solution)/shard_map/jit(_cho_solve)/triangular_solve | solution.py:50
  902.1 12.5 %convolution_subtract_fusion.2 = f32[256,4096]{1,0:T(8,128)S(1)} fusion(f32[256,4096]{1,0:T(8,128)} %copy-done.1, f32[2,4096,256]{2,1,0:T(8,128)} %all-gather.11.cloned.1.call-done, f32[128,256]{1,0:T(8,128)S(1)} %convolution_negate_fusion, f32[128,256]{1,0:T(8,128)S(1)} %fusion.108), kind=kOutput, calls=%fused_computation.28 | convolution fusion | flops 3222339584 | bytes 12845056 | tf_op jit(solution)/shard_map/dot_general | solution.py:23
  (289 shorter events, 192.5 us)
Async XLA Ops:
  7.2 169.6 %all-gather.5.cloned.1.call-start = ((), (), s32[]{:S(2)}) async-start(), calls=%async_computation | async-start | bytes 4456448 | tf_op jit(solution)/shard_map/all_gather | solution.py:56
  13.8 333.1 %all-gather.9.cloned.1.call-start = ((), (), s32[]{:S(2)}) async-start(), calls=%async_computation.2 | async-start | bytes 4456448 | tf_op jit(solution)/shard_map/all_gather | solution.py:56
  16.2 361.3 %all-reduce.9.cloned.1.call-start = ((), (), s32[]{:S(2)}) async-start(), calls=%async_computation.5 | async-start | bytes 1048576 | tf_op jit(solution)/shard_map/psum | solution.py:66
  26.9 210.2 %copy-start.22 = (s32[1,512]{1,0:T(1,128)}, s32[1,512]{1,0:T(1,128)S(1)}, u32[]{:S(2)}) copy-start(s32[1,512]{1,0:T(1,128)S(1)} %get-tuple-element.132) | copy-start | bytes 6148
  26.9 44.0 %copy-start.11 = (f32[256,4096]{1,0:T(8,128)S(1)}, f32[256,4096]{1,0:T(8,128)}, u32[]{:S(2)}) copy-start(f32[256,4096]{1,0:T(8,128)} %fusion.359) | copy-start | bytes 12582916
  70.9 52.9 %copy-start.10 = (f32[256,4096]{1,0:T(8,128)S(1)}, f32[256,4096]{1,0:T(8,128)}, u32[]{:S(2)}) copy-start(f32[256,4096]{1,0:T(8,128)} %fusion.363) | copy-start | bytes 12582916
  210.1 16.8 %slice-start = ((s8[8388608]{0:T(1024)(128)(4,1)}), s8[4194304]{0:T(1024)(128)(4,1)S(1)}, s32[]{:S(2)}) async-start(s8[8388608]{0:T(1024)(128)(4,1)} %bitcast.344), calls=%async_computation.6 | async-start | bytes 8388608
  215.8 11.1 %slice-start.1 = ((s8[8388608]{0:T(1024)(128)(4,1)}), s8[4194304]{0:T(1024)(128)(4,1)S(1)}, s32[]{:S(2)}) async-start(s8[8388608]{0:T(1024)(128)(4,1)} %bitcast.344), calls=%async_computation.7 | async-start | bytes 8388608
  232.1 291.9 %all-gather.7.cloned.1.call-start = ((), (), s32[]{:S(2)}) async-start(), calls=%async_computation.1 | async-start | bytes 8912896 | tf_op jit(solution)/shard_map/all_gather | solution.py:71
  234.5 535.2 %all-reduce.7.cloned.1.call-start = ((), (), s32[]{:S(2)}) async-start(), calls=%async_computation.4 | async-start | bytes 1048576 | tf_op jit(solution)/shard_map/psum | solution.py:66
  237.1 68.7 %copy-start.19 = (f32[256,512]{1,0:T(8,128)S(1)}, f32[256,512]{1,0:T(8,128)}, u32[]{:S(2)}) copy-start(f32[256,512]{1,0:T(8,128)} %fusion.71) | copy-start | bytes 1572868
  237.1 68.7 %copy-start.28 = (f32[512,256]{0,1:T(8,128)S(1)}, f32[512,256]{0,1:T(8,128)}, u32[]{:S(2)}) copy-start(f32[512,256]{0,1:T(8,128)} %fusion.12) | copy-start | bytes 1572868
  305.8 41.1 %copy-start.12 = (f32[256,256]{1,0:T(8,128)S(1)}, f32[256,256]{1,0:T(8,128)}, u32[]{:S(2)}) copy-start(f32[256,256]{1,0:T(8,128)} %get-tuple-element.141) | copy-start | bytes 786436
  420.5 22.0 %copy-start.26 = (s32[2,2]{1,0:T(2,128)}, s32[2,2]{1,0:T(2,128)S(1)}, u32[]{:S(2)}) copy-start(s32[2,2]{1,0:T(2,128)S(1)} %get-tuple-element.380) | copy-start | bytes 52
  531.7 45.2 %slice-start.2 = ((s8[8388608]{0:T(1024)(128)(4,1)}), s8[4194304]{0:T(1024)(128)(4,1)S(1)}, s32[]{:S(2)}) async-start(s8[8388608]{0:T(1024)(128)(4,1)} %bitcast.346), calls=%async_computation.8 | async-start | bytes 8388608
  535.6 53.5 %copy-start.1 = (f32[256,4096]{1,0:T(8,128)}, f32[256,4096]{1,0:T(8,128)S(1)}, u32[]{:S(2)}) copy-start(f32[256,4096]{1,0:T(8,128)S(1)} %convolution_subtract_fusion.4) | copy-start | bytes 12582916
  535.6 41.3 %slice-start.3 = ((s8[8388608]{0:T(1024)(128)(4,1)}), s8[4194304]{0:T(1024)(128)(4,1)S(1)}, s32[]{:S(2)}) async-start(s8[8388608]{0:T(1024)(128)(4,1)} %bitcast.346), calls=%async_computation.9 | async-start | bytes 8388608
  594.1 308.0 %all-gather.11.cloned.1.call-start = ((), (), s32[]{:S(2)}) async-start(), calls=%async_computation.3 | async-start | bytes 8912896 | tf_op jit(solution)/shard_map/all_gather | solution.py:71
  594.2 44.5 %copy-start.14 = (f32[256,256]{0,1:T(8,128)}, f32[256,256]{0,1:T(8,128)S(1)}, u32[]{:S(2)}) copy-start(f32[256,256]{0,1:T(8,128)S(1)} %negate_bitcast_fusion) | copy-start | bytes 786436
  595.2 43.5 %copy-start.4 = (f32[256,4096]{1,0:T(8,128)S(1)}, f32[256,4096]{1,0:T(8,128)}, u32[]{:S(2)}) copy-start(f32[256,4096]{1,0:T(8,128)} %copy-done.3) | copy-start | bytes 12582916
  595.2 43.5 %copy-start.29 = (f32[256,512]{1,0:T(8,128)S(1)}, f32[256,512]{1,0:T(8,128)}, u32[]{:S(2)}) copy-start(f32[256,512]{1,0:T(8,128)} %fusion.30) | copy-start | bytes 1572868
  638.7 38.5 %copy-start.2 = (f32[256,4096]{1,0:T(8,128)S(1)}, f32[256,4096]{1,0:T(8,128)}, u32[]{:S(2)}) copy-start(f32[256,4096]{1,0:T(8,128)} %copy-done.1) | copy-start | bytes 12582916
  677.2 53.5 %copy-start.25 = (f32[512]{0:T(512)S(1)}, f32[512]{0:T(512)}, u32[]{:S(2)}) copy-start(f32[512]{0:T(512)} %get-tuple-element.159) | copy-start | bytes 6148
  677.2 90.5 %copy-start.20 = (f32[256,512]{1,0:T(8,128)S(1)}, f32[256,512]{1,0:T(8,128)}, u32[]{:S(2)}) copy-start(f32[256,512]{1,0:T(8,128)} %fusion.71) | copy-start | bytes 1572868
  677.2 90.5 %copy-start.21 = (f32[256,512]{1,0:T(8,128)S(1)}, f32[256,512]{1,0:T(8,128)}, u32[]{:S(2)}) copy-start(f32[256,512]{1,0:T(8,128)} %get-tuple-element.160) | copy-start | bytes 1572868
  767.7 40.6 %copy-start.27 = (s32[2,2]{1,0:T(2,128)S(1)}, s32[2,2]{1,0:T(2,128)}, u32[]{:S(2)}) copy-start(s32[2,2]{1,0:T(2,128)} %get-tuple-element.381) | copy-start | bytes 52
  767.9 64.9 %slice-start.4 = ((f32[256,256]{0,1:T(8,128)}), f32[128,256]{0,1:T(8,128)S(1)}, s32[]{:S(2)}) async-start(f32[256,256]{0,1:T(8,128)} %copy-done.14), calls=%async_computation.10 | async-start | bytes 262144 | tf_op jit(solution)/shard_map/slice | solution.py:89
  769.7 129.3 %copy-start.15 = (f32[256,256]{0,1:T(8,128)S(1)}, f32[256,256]{0,1:T(8,128)}, u32[]{:S(2)}) copy-start(f32[256,256]{0,1:T(8,128)} %copy-done.14) | copy-start | bytes 786436
  769.7 66.1 %copy-start.16 = (f32[256,256]{0,1:T(8,128)S(1)}, f32[256,256]{0,1:T(8,128)}, u32[]{:S(2)}) copy-start(f32[256,256]{0,1:T(8,128)} %get-tuple-element.73) | copy-start | bytes 786436
  769.7 66.4 %copy-start.18 = (f32[256,256]{0,1:T(8,128)S(1)}, f32[256,256]{0,1:T(8,128)}, u32[]{:S(2)}) copy-start(f32[256,256]{0,1:T(8,128)} %get-tuple-element.74) | copy-start | bytes 786436
  902.1 12.5 %copy-start.5 = (f32[256,4096]{1,0:T(8,128)S(1)}, f32[256,4096]{1,0:T(8,128)}, u32[]{:S(2)}) copy-start(f32[256,4096]{1,0:T(8,128)} %copy-done.3) | copy-start | bytes 12582916
  902.1 12.5 %copy-start.6 = (f32[2,4096,256]{2,1,0:T(8,128)S(1)}, f32[2,4096,256]{2,1,0:T(8,128)}, u32[]{:S(2)}) copy-start(f32[2,4096,256]{2,1,0:T(8,128)} %all-gather.11.cloned.1.call-done) | copy-start | bytes 25165828
  (9 other events, 48.8 us)
Sparse Core Ops, SparseCore 0:
  13.9 67.0 all-gather.4
  83.1 62.5 all-gather.8
  232.3 93.4 all-reduce.8
  327.7 78.2 all-gather.6
  594.3 93.5 all-reduce.6
  689.9 75.3 all-gather.10
where the time goes:
time: 954 us; the launch traced here: 946 us
  matrix products  478 us (50%)
  other arithmetic  306 us (32%)
  local copies, waits for them, and re-layouts  104 us (11%)
  blocking collectives  36.4 us (4%)
  between operations  21 us (2%)
    dot_general x40, matrix products, matmul(): jnp.dot(left, right, precision=precise, preferred_element_type=jnp.float32)  408 us
    another operation x28, other arithmetic, hermitian_solve(): factor = jnp.linalg.cholesky(embedded)  139 us
    another operation x9, other arithmetic, hermitian_solve(): jax.scipy.linalg.cho_solve((factor, True), jnp.concatenate([rhs_re, rhs_i...  80.9 us
    cos x1, other arithmetic, steering(): return (jnp.cos(phase), jnp.sin(phase))  68.7 us
    slice x6, local copies, waits for them, and re-layouts, block_product(): new_re = matmul(inv_re, piece_wide[0]) - matmul(inv_im, piece_wide[1])  63.9 us
    dot_general x8, matrix products, tail_dot(): lax.dot_general(left, right, (((1,), (1,)), ((), ())), precision=precise,...  52.1 us
    psum x1, blocking collectives, on_device(): power = lax.psum(partial_power, 'row')  36.4 us
  transfers between devices with their start and end apart: 6, of which 0 were waited for; matrix products, arithmetic and copies ran while one was open for 82% of the time, Pallas kernels for 0%

commit v1 on v0

--- a/solution.py
+++ b/solution.py
@@ -115,7 +115,11 @@
         local_im = lax.dynamic_slice_in_dim(steer_im, first_row, row_count, 0)
         app_re, app_im = complex_mul(current[0], current[1], steer_re, steer_im)
         partial_power = jnp.sum(local_re * app_re + local_im * app_im, axis=0)
-        power = lax.psum(partial_power, "row")
+
+        def sections_fit(mine_x):
+            return lax.all_gather(mine_x, "row").sum(axis=0)
+
+        power = sections_fit(partial_power)
         departed = jnp.take(cycle, departing[step_index], axis=2)
         current = joint_update(current, jnp.concatenate([arrivals[step_index], departed], axis=2))
         weight_list.append(jnp.stack([M * app_re / power, M * app_im / power]))

time: 954 us -> 1000 us (1.048)
  matrix products: 478 us -> 499 us
  other arithmetic: 306 us -> 317 us
  local copies, waits for them, and re-layouts: 104 us -> 115 us
    all_gather x0 -> x2, blocking collectives: none -> 41.3 us  [sections_fit(): return lax.all_gather(mine_x, 'row').sum(axis=0)]
    psum x1 -> x0, blocking collectives: 36.4 us -> none  [on_device(): power = lax.psum(partial_power, 'row')]
    dot_general x40, matrix products: 408 us -> 420 us  [matmul(): jnp.dot(left, right, precision=precise, preferred_element_type=jnp.float32)]
  transfers between devices with their start and end apart: 6 -> 6, of which waited for: 0 -> 0; matrix products, arithmetic and copies ran while one was open for 82% -> 86% of each run, Pallas kernels for 0% -> 0%
where the time goes in v1:
time: 1000 us; the launch traced here: 994 us
  matrix products  499 us (50%)
  other arithmetic  317 us (32%)
  local copies, waits for them, and re-layouts  115 us (12%)
  blocking collectives  41.3 us (4%)
  between operations  20.9 us (2%)
    dot_general x40, matrix products, matmul(): jnp.dot(left, right, precision=precise, preferred_element_type=jnp.float32)  420 us
    another operation x28, other arithmetic, hermitian_solve(): factor = jnp.linalg.cholesky(embedded)  146 us
    another operation x9, other arithmetic, hermitian_solve(): jax.scipy.linalg.cho_solve((factor, True), jnp.concatenate([rhs_re, rhs_i...  82.3 us
    cos x1, other arithmetic, steering(): return (jnp.cos(phase), jnp.sin(phase))  68.7 us
    slice x6, local copies, waits for them, and re-layouts, block_product(): new_re = matmul(inv_re, piece_wide[0]) - matmul(inv_im, piece_wide[1])  64.1 us
    dot_general x8, matrix products, tail_dot(): lax.dot_general(left, right, (((1,), (1,)), ((), ())), precision=precise,...  51.8 us
    all_gather x2, blocking collectives, sections_fit(): return lax.all_gather(mine_x, 'row').sum(axis=0)  41.3 us
  transfers between devices with their start and end apart: 6, of which 0 were waited for; matrix products, arithmetic and copies ran while one was open for 86% of the time, Pallas kernels for 0%

profile of v1, /device:TPU:0, one launch (start us, length us, event | category | flops | bytes accessed | tf_op | source)
XLA Modules:
  0.0 993.7 jit_solution(4882424606158126414)
XLA Ops:
  26.9 44.0 %fusion.14 = f32[512,256]{0,1:T(8,128)S(1)} fusion(s32[4096]{0:T(1024)S(1)} %iota_multiply_fusion, s32[512]{0:T(512)S(1)} %bitcast.365, f32[256,4096]{1,0:T(8,128)} %fusion.361), kind=kOutput, calls=%fused_computation.43 | convolution fusion | flops 6473908224 | bytes 4737024 | tf_op jit(solution)/shard_map/dot_general | solution.py:13
  70.9 52.9 %fusion.12 = f32[512,256]{0,1:T(8,128)} fusion(s32[4096]{0:T(1024)S(1)} %iota_multiply_fusion, s32[512]{0:T(512)S(1)} %bitcast.366, f32[256,4096]{1,0:T(8,128)S(1)} %copy-done.12), kind=kOutput, calls=%fused_computation.41 | convolution fusion | flops 6473908224 | bytes 4737024 | tf_op jit(solution)/shard_map/dot_general | solution.py:13
  123.8 52.9 %fusion.71 = f32[256,512]{1,0:T(8,128)} fusion(f32[512,256]{0,1:T(8,128)S(1)} %fusion.14, s32[4096]{0:T(1024)S(1)} %iota_multiply_fusion, s32[512]{0:T(512)S(1)} %bitcast.367, f32[256,4096]{1,0:T(8,128)S(1)} %copy-done.11), kind=kOutput, calls=%fused_computation.85 | convolution fusion | flops 6474039296 | bytes 5261312 | tf_op jit(solution)/shard_map/dot_general | solution.py:13
  176.7 14.5 %fusion.275 = (bf16[1,4096,256]{1,0,2:T(2,128)(2,1)}, bf16[1,4096,256]{1,0,2:T(2,128)(2,1)}) fusion(bf16[2,4096,256]{1,0,2:T(2,128)(2,1)} %all-gather.9.cloned.1.call-done), kind=kLoop, calls=%fused_computation.391 | loop fusion | bytes 8388608 | tf_op jit(solution)/shard_map/slice | solution.py:57
  191.2 9.7 copy.83
  239.5 68.7 %fusion.11 = (f32[4096,512]{1,0:T(8,128)S(1)}, f32[4096,512]{1,0:T(8,128)S(1)}, f32[4096,512]{1,0:T(8,128)}, f32[4096,512]{1,0:T(8,128)}) fusion(s32[4096]{0:T(1024)S(1)} %iota_multiply_fusion, s32[512]{0:T(512)S(1)} %bitcast.368, s32[512]{0:T(512)S(1)} %bitcast.360), kind=kLoop, calls=%fused_computation.36 | loop fusion | flops 62914560 | bytes 33574912 | tf_op jit(solution)/shard_map/cos | solution.py:41
  308.2 39.4 %add_reduce_fusion.1 = (f32[512]{0:T(512)S(1)}, f32[256,512]{1,0:T(8,128)S(1)}) fusion(f32[4096,512]{1,0:T(8,128)S(1)} %get-tuple-element.124, s32[]{:T(128)S(6)} %select_n.28, f32[256,512]{1,0:T(8,128)S(1)} %copy-done.30, f32[4096,512]{1,0:T(8,128)S(1)} %get-tuple-element.123, f32[512,256]{0,1:T(8,128)S(1)} %copy-done.38, ...), kind=kOutput, calls=%fused_computation.143 | convolution fusion | flops 6474563072 | bytes 6836228 | tf_op jit(solution)/shard_map/dot_general | solution.py:13
  347.7 23.7 %all-gather.2 = f32[16,1,512]{2,1,0:T(1,128)S(1)} all-gather(f32[1,1,512]{2,1,0:T(1,128)S(1)} %bitcast.373), channel_id=2, replica_groups=mesh['groups'=2,'row'=16] {'row'}, dimensions={0}, use_global_device_ids=true | all-gather | bytes 34816 | tf_op jit(solution)/shard_map/all_gather | solution.py:120
  374.7 11.6 %fusion.274 = (bf16[1,4096,256]{1,0,2:T(2,128)(2,1)}, bf16[1,4096,256]{1,0,2:T(2,128)(2,1)}) fusion(bf16[2,4096,256]{1,0,2:T(2,128)(2,1)} %all-gather.13.cloned.1.call-done), kind=kLoop, calls=%fused_computation.390 | loop fusion | bytes 8388608 | tf_op jit(solution)/shard_map/slice | solution.py:57
  395.6 9.8 copy.97
  409.4 11.7 %cholesky.214 = f32[128,128]{1,0:T(8,128)S(1)} custom-call(f32[128,128]{1,0:T(8,128)S(1)} %cholesky.346), custom_call_target="Cholesky" | custom-call | tf_op jit(solution)/shard_map/jit(cholesky)/cholesky | solution.py:49
  421.1 9.8 custom-call.23
  433.1 11.7 %cholesky.231 = f32[128,128]{1,0:T(8,128)S(1)} custom-call(f32[128,128]{1,0:T(8,128)S(1)} %convolution_subtract_fusion.25), custom_call_target="Cholesky" | custom-call | tf_op jit(solution)/shard_map/jit(cholesky)/cholesky | solution.py:49
  452.9 20.1 %custom-call.24 = f32[2,128,128]{1,2,0:T(8,128)S(1)} custom-call(f32[2,128,128]{2,1,0:T(8,128)S(1)} %get-tuple-element.35), custom_call_target="InvertDiagBlocksLowerTriangular" | custom-call | tf_op jit(solution)/shard_map/jit(_cho_solve)/triangular_solve | solution.py:50
  489.9 12.3 %cholesky.248 = f32[128,128]{1,0:T(8,128)} custom-call(f32[128,128]{1,0:T(8,128)S(1)} %cholesky.349), custom_call_target="Cholesky" | custom-call | tf_op jit(solution)/shard_map/jit(cholesky)/cholesky | solution.py:49
  505.1 11.3 %custom-call.25 = f32[1,128,128]{1,2,0:T(8,128)} custom-call(f32[1,128,128]{2,1,0:T(8,128)} %get-tuple-element.118), custom_call_target="InvertDiagBlocksLowerTriangular" | custom-call | tf_op jit(solution)/shard_map/jit(cholesky)/cholesky | solution.py:49
  519.2 13.3 %cholesky.265 = f32[128,128]{1,0:T(8,128)} custom-call(f32[128,128]{1,0:T(8,128)} %convolution_subtract_fusion.23), custom_call_target="Cholesky" | custom-call | tf_op jit(solution)/shard_map/jit(cholesky)/cholesky | solution.py:49
  544.8 21.1 %custom-call.26 = f32[2,128,128]{1,2,0:T(8,128)} custom-call(f32[2,128,128]{2,1,0:T(8,128)} %get-tuple-element.36), custom_call_target="InvertDiagBlocksLowerTriangular" | custom-call | tf_op jit(solution)/shard_map/jit(_cho_solve)/triangular_solve | solution.py:50
  610.2 43.5 %fusion.30 = f32[256,512]{1,0:T(8,128)S(1)} fusion(f32[256,4096]{1,0:T(8,128)} %copy-done.1, s32[512]{0:T(512)S(1)} %bitcast.361, s32[4096]{0:T(1024)S(1)} %iota_multiply_fusion), kind=kOutput, calls=%fused_computation.58 | convolution fusion | flops 6473908224 | bytes 4737024 | tf_op jit(solution)/shard_map/dot_general | solution.py:13
  653.8 52.0 %fusion.28 = f32[256,512]{1,0:T(8,128)S(1)} fusion(f32[256,4096]{1,0:T(8,128)S(1)} %copy-done.4, s32[512]{0:T(512)S(1)} %bitcast.362, s32[4096]{0:T(1024)S(1)} %iota_multiply_fusion), kind=kOutput, calls=%fused_computation.57 | convolution fusion | flops 6473908224 | bytes 4737024 | tf_op jit(solution)/shard_map/dot_general | solution.py:13
  705.8 38.3 %fusion.60 = f32[256,512]{1,0:T(8,128)S(1)} fusion(f32[256,512]{1,0:T(8,128)S(1)} %fusion.30, f32[256,4096]{1,0:T(8,128)S(1)} %copy-done.4, s32[512]{0:T(512)S(1)} %bitcast.363, s32[4096]{0:T(1024)S(1)} %iota_multiply_fusion), kind=kOutput, calls=%fused_computation.82 | convolution fusion | flops 6474039296 | bytes 5261312 | tf_op jit(solution)/shard_map/dot_general | solution.py:13
  744.2 53.5 %add_reduce_fusion = (f32[512]{0:T(512)S(1)}, f32[256,512]{1,0:T(8,128)S(1)}) fusion(f32[4096,512]{1,0:T(8,128)} %get-tuple-element.127, s32[]{:T(128)S(6)} %select_n.28, f32[256,512]{1,0:T(8,128)S(1)} %fusion.60, f32[4096,512]{1,0:T(8,128)} %get-tuple-element.128, f32[256,512]{1,0:T(8,128)S(1)} %fusion.28, f32[256,4096]{1,0:T(8,128)S(1)} %copy-done.2, ...), kind=kOutput, calls=%fused_computation.140 | convolution fusion | flops 6474563072 | bytes 6836228 | tf_op jit(solution)/shard_map/dot_general | solution.py:13
  797.7 17.7 %all-gather.3 = f32[16,1,512]{2,1,0:T(1,128)S(1)} all-gather(f32[1,1,512]{2,1,0:T(1,128)S(1)} %bitcast.372), channel_id=3, replica_groups=mesh['groups'=2,'row'=16] {'row'}, dimensions={0}, use_global_device_ids=true | all-gather | bytes 34816 | tf_op jit(solution)/shard_map/all_gather | solution.py:120
  819.9 11.7 %cholesky.282 = f32[128,128]{1,0:T(8,128)S(1)} custom-call(f32[128,128]{1,0:T(8,128)S(1)} %cholesky.352), custom_call_target="Cholesky" | custom-call | tf_op jit(solution)/shard_map/jit(cholesky)/cholesky | solution.py:49
  831.7 9.8 custom-call.27
  842.0 11.7 %cholesky.299 = f32[128,128]{1,0:T(8,128)S(1)} custom-call(f32[128,128]{1,0:T(8,128)S(1)} %convolution_subtract_fusion.22), custom_call_target="Cholesky" | custom-call | tf_op jit(solution)/shard_map/jit(cholesky)/cholesky | solution.py:49
  860.3 19.8 %custom-call.28 = f32[2,128,128]{1,2,0:T(8,128)S(1)} custom-call(f32[2,128,128]{2,1,0:T(8,128)S(1)} %get-tuple-element.37), custom_call_target="InvertDiagBlocksLowerTriangular" | custom-call | tf_op jit(solution)/shard_map/jit(_cho_solve)/triangular_solve | solution.py:50
  884.8 11.7 %cholesky.316 = f32[128,128]{1,0:T(8,128)S(1)} custom-call(f32[128,128]{1,0:T(8,128)S(1)} %cholesky.355), custom_call_target="Cholesky" | custom-call | tf_op jit(solution)/shard_map/jit(cholesky)/cholesky | solution.py:49
  896.6 9.8 custom-call.29
  906.9 11.9 %cholesky.333 = f32[128,128]{1,0:T(8,128)S(1)} custom-call(f32[128,128]{1,0:T(8,128)S(1)} %convolution_subtract_fusion.20), custom_call_target="Cholesky" | custom-call | tf_op jit(solution)/shard_map/jit(cholesky)/cholesky | solution.py:49
  925.4 19.7 %custom-call.30 = f32[2,128,128]{1,2,0:T(8,128)S(1)} custom-call(f32[2,128,128]{2,1,0:T(8,128)S(1)} %get-tuple-element.38), custom_call_target="InvertDiagBlocksLowerTriangular" | custom-call | tf_op jit(solution)/shard_map/jit(_cho_solve)/triangular_solve | solution.py:50
  949.7 12.5 %convolution_subtract_fusion.2 = f32[256,4096]{1,0:T(8,128)S(1)} fusion(f32[256,4096]{1,0:T(8,128)} %copy-done.1, f32[2,4096,256]{2,1,0:T(8,128)} %all-gather.15.cloned.1.call-done, f32[128,256]{1,0:T(8,128)S(1)} %convolution_negate_fusion, f32[128,256]{1,0:T(8,128)S(1)} %fusion.108), kind=kOutput, calls=%fused_computation.28 | convolution fusion | flops 3222339584 | bytes 12845056 | tf_op jit(solution)/shard_map/dot_general | solution.py:23
  (310 shorter events, 229.2 us)
Async XLA Ops:
  7.2 169.6 %all-gather.9.cloned.1.call-start = ((), (), s32[]{:S(2)}) async-start(), calls=%async_computation | async-start | bytes 4456448 | tf_op jit(solution)/shard_map/all_gather | solution.py:56
  13.8 360.9 %all-gather.13.cloned.1.call-start = ((), (), s32[]{:S(2)}) async-start(), calls=%async_computation.2 | async-start | bytes 4456448 | tf_op jit(solution)/shard_map/all_gather | solution.py:56
  16.2 389.2 %all-reduce.8.cloned.1.call-start = ((), (), s32[]{:S(2)}) async-start(), calls=%async_computation.5 | async-start | bytes 1048576 | tf_op jit(solution)/shard_map/psum | solution.py:66
  26.9 212.6 %copy-start.32 = (s32[1,512]{1,0:T(1,128)}, s32[1,512]{1,0:T(1,128)S(1)}, u32[]{:S(2)}) copy-start(s32[1,512]{1,0:T(1,128)S(1)} %get-tuple-element.130) | copy-start | bytes 6148
  26.9 44.0 %copy-start.12 = (f32[256,4096]{1,0:T(8,128)S(1)}, f32[256,4096]{1,0:T(8,128)}, u32[]{:S(2)}) copy-start(f32[256,4096]{1,0:T(8,128)} %fusion.359) | copy-start | bytes 12582916
  70.9 52.9 %copy-start.11 = (f32[256,4096]{1,0:T(8,128)S(1)}, f32[256,4096]{1,0:T(8,128)}, u32[]{:S(2)}) copy-start(f32[256,4096]{1,0:T(8,128)} %fusion.363) | copy-start | bytes 12582916
  210.2 16.1 %slice-start = ((s8[8388608]{0:T(1024)(128)(4,1)}), s8[4194304]{0:T(1024)(128)(4,1)S(1)}, s32[]{:S(2)}) async-start(s8[8388608]{0:T(1024)(128)(4,1)} %bitcast.346), calls=%async_computation.6 | async-start | bytes 8388608
  215.9 10.4 %slice-start.1 = ((s8[8388608]{0:T(1024)(128)(4,1)}), s8[4194304]{0:T(1024)(128)(4,1)S(1)}, s32[]{:S(2)}) async-start(s8[8388608]{0:T(1024)(128)(4,1)} %bitcast.346), calls=%async_computation.7 | async-start | bytes 8388608
  215.9 10.4 %copy-start.8 = (bf16[1,4096,256]{2,1,0:T(8,128)(2,1)S(1)}, bf16[1,4096,256]{2,1,0:T(8,128)(2,1)}, u32[]{:S(2)}) copy-start(bf16[1,4096,256]{2,1,0:T(8,128)(2,1)} %copy.83) | copy-start | bytes 6291460
  221.0 153.1 %copy-start.18 = (f32[256,256]{1,0:T(8,128)}, f32[256,256]{1,0:T(8,128)S(1)}, u32[]{:S(2)}) copy-start(f32[256,256]{1,0:T(8,128)S(1)} %get-tuple-element.139) | copy-start | bytes 786436
  231.6 346.6 %all-gather.11.cloned.1.call-start = ((), (), s32[]{:S(2)}) async-start(), calls=%async_computation.1 | async-start | bytes 8912896 | tf_op jit(solution)/shard_map/all_gather | solution.py:71
  237.1 580.7 %all-reduce.6.cloned.1.call-start = ((), (), s32[]{:S(2)}) async-start(), calls=%async_computation.4 | async-start | bytes 1048576 | tf_op jit(solution)/shard_map/psum | solution.py:66
  239.5 68.7 %copy-start.10 = (f32[256,4096]{1,0:T(8,128)S(1)}, f32[256,4096]{1,0:T(8,128)}, u32[]{:S(2)}) copy-start(f32[256,4096]{1,0:T(8,128)} %fusion.84.clone.5) | copy-start | bytes 12582916
  239.5 68.7 %copy-start.30 = (f32[256,512]{1,0:T(8,128)S(1)}, f32[256,512]{1,0:T(8,128)}, u32[]{:S(2)}) copy-start(f32[256,512]{1,0:T(8,128)} %fusion.71) | copy-start | bytes 1572868
  239.5 68.7 %copy-start.38 = (f32[512,256]{0,1:T(8,128)S(1)}, f32[512,256]{0,1:T(8,128)}, u32[]{:S(2)}) copy-start(f32[512,256]{0,1:T(8,128)} %fusion.12) | copy-start | bytes 1572868
  575.5 10.0 %copy-start.14 = (f32[128,256]{1,0:T(8,128)S(1)}, f32[128,256]{1,0:T(8,128)}, u32[]{:S(2)}) copy-start(f32[128,256]{1,0:T(8,128)} %get-tuple-element.145) | copy-start | bytes 393220
  578.1 7.4 copy-start.6
  589.4 14.6 %copy-start.1 = (f32[256,4096]{1,0:T(8,128)}, f32[256,4096]{1,0:T(8,128)S(1)}, u32[]{:S(2)}) copy-start(f32[256,4096]{1,0:T(8,128)S(1)} %convolution_subtract_fusion.4) | copy-start | bytes 12582916
  599.5 6.7 copy-start.3
  601.5 7.7 copy-start.13
  609.2 340.5 %all-gather.15.cloned.1.call-start = ((), (), s32[]{:S(2)}) async-start(), calls=%async_computation.3 | async-start | bytes 8912896 | tf_op jit(solution)/shard_map/all_gather | solution.py:71
  610.2 43.5 %copy-start.4 = (f32[256,4096]{1,0:T(8,128)S(1)}, f32[256,4096]{1,0:T(8,128)}, u32[]{:S(2)}) copy-start(f32[256,4096]{1,0:T(8,128)} %copy-done.3) | copy-start | bytes 12582916
  653.8 52.1 %copy-start.20 = (f32[256,256]{0,1:T(8,128)}, f32[256,256]{0,1:T(8,128)S(1)}, u32[]{:S(2)}) copy-start(f32[256,256]{0,1:T(8,128)S(1)} %negate_bitcast_fusion) | copy-start | bytes 786436
  705.8 38.3 %copy-start.2 = (f32[256,4096]{1,0:T(8,128)S(1)}, f32[256,4096]{1,0:T(8,128)}, u32[]{:S(2)}) copy-start(f32[256,4096]{1,0:T(8,128)} %copy-done.1) | copy-start | bytes 12582916
  744.2 71.2 %copy-start.34 = (f32[512]{0:T(512)S(1)}, f32[512]{0:T(512)}, u32[]{:S(2)}) copy-start(f32[512]{0:T(512)} %broadcast_divide_fusion.1) | copy-start | bytes 6148
  797.7 58.6 %copy-start.37 = (s32[2,2]{1,0:T(2,128)S(1)}, s32[2,2]{1,0:T(2,128)}, u32[]{:S(2)}) copy-start(s32[2,2]{1,0:T(2,128)} %get-tuple-element.379) | copy-start | bytes 52
  797.7 82.9 %slice-start.4 = ((f32[256,256]{0,1:T(8,128)}), f32[128,256]{0,1:T(8,128)S(1)}, s32[]{:S(2)}) async-start(f32[256,256]{0,1:T(8,128)} %copy-done.20), calls=%async_computation.10 | async-start | bytes 262144 | tf_op jit(solution)/shard_map/slice | solution.py:89
  817.8 128.8 %copy-start.21 = (f32[256,256]{0,1:T(8,128)S(1)}, f32[256,256]{0,1:T(8,128)}, u32[]{:S(2)}) copy-start(f32[256,256]{0,1:T(8,128)} %copy-done.20) | copy-start | bytes 786436
  817.8 65.8 %copy-start.22 = (f32[256,256]{0,1:T(8,128)S(1)}, f32[256,256]{0,1:T(8,128)}, u32[]{:S(2)}) copy-start(f32[256,256]{0,1:T(8,128)} %get-tuple-element.71) | copy-start | bytes 786436
  817.8 66.2 %copy-start.25 = (f32[256,256]{0,1:T(8,128)S(1)}, f32[256,256]{0,1:T(8,128)}, u32[]{:S(2)}) copy-start(f32[256,256]{0,1:T(8,128)} %get-tuple-element.72) | copy-start | bytes 786436
  949.7 12.5 %copy-start.5 = (f32[256,4096]{1,0:T(8,128)S(1)}, f32[256,4096]{1,0:T(8,128)}, u32[]{:S(2)}) copy-start(f32[256,4096]{1,0:T(8,128)} %copy-done.3) | copy-start | bytes 12582916
  949.7 12.5 %copy-start.7 = (f32[2,4096,256]{2,1,0:T(8,128)S(1)}, f32[2,4096,256]{2,1,0:T(8,128)}, u32[]{:S(2)}) copy-start(f32[2,4096,256]{2,1,0:T(8,128)} %all-gather.15.cloned.1.call-done) | copy-start | bytes 25165828
  (18 other events, 62.6 us)
Sparse Core Ops, SparseCore 0:
  13.9 67.0 all-gather.8
  83.1 62.5 all-gather.12
  231.7 93.4 all-reduce.7
  327.1 78.2 all-gather.10
  609.3 88.1 all-reduce.5
  699.6 74.8 all-gather.14
